TPU v7x, 512 devices: a whole 4x8x8 slice. The times are simulated.
512 devices in a mesh: lat: 32 (over z, y_hi, core), lon: 16 (over y_lo, x).
Axes of the slice: x: 4, y: 8 (y_hi: 2, y_lo: 4; y = y_hi * 4 + y_lo), z: 8, core: 2. Of those that a mesh axis runs over, the one named last changes fastest.
Arguments:
- fields: float32 [5, 32, 32, 4096], P(None, None, 'lat', 'lon'), may hold values from -6 to 6
- east_courant: float32 [32, 32, 4096], P(None, 'lat', 'lon'), may hold values from -0.45 to 0.45
- north_courant: float32 [32, 32, 4096], P(None, 'lat', 'lon'), may hold values from -0.45 to 0.45
- offsets: int32 [32], P('lat'), may hold values from -8 to 7
- lower_blocks: float32 [5, 5, 31, 32], P(None, None, None, 'lat'), may hold values from -0.4 to 0.4
- pivot_inverse: float32 [5, 5, 32, 32], P(None, None, None, 'lat'), may hold values from -0.36 to 1, as said below
- upper_blocks: float32 [5, 5, 31, 32], P(None, None, None, 'lat'), may hold values from -0.4 to 0.4
Outputs:
- solved: float32 [5, 32, 32, 4096], P(None, None, 'lat', 'lon')
Inputs may be any that keep to these rules, and one draw needn't show every extreme that they name: `pivot_inverse`: diagonal entries of each 5 x 5 block lie between 0.3 and 1; off-diagonal entries are at most 0.36 in magnitude.
All inputs are finite; a program needn't handle non-finite values.
Results may differ from a plain program's by a relative error of at most 0.0001.
Values sent between devices are 32-bit elements; how exact they have to be, the bound alone decides.
A program may use at most 64 MiB of HBM per device.

v0:
```python
import jax
import jax.numpy as jnp
from jax import lax
from jax.sharding import PartitionSpec as P


def padded(block, sides, width, periodic):
    for axis, dim in sides:
        count = lax.axis_size(axis)
        forward = [(i, i + 1) for i in range(count - 1)]
        if periodic:
            forward.append((count - 1, 0))
        backward = [(target, source) for source, target in forward]
        low = lax.ppermute(
            lax.slice_in_dim(block, block.shape[dim] - width, None, axis=dim), axis, forward
        )
        high = lax.ppermute(lax.slice_in_dim(block, 0, width, axis=dim), axis, backward)
        block = jnp.concatenate([low, block, high], axis=dim)
    return block


def apply_block(block, vector):
    return jnp.einsum("abj,bji->aji", block, vector, precision=lax.Precision.HIGHEST)


def column_solve(advected, lower_blocks, pivot_inverse, upper_blocks):
    first = apply_block(pivot_inverse[:, :, 0], advected[:, 0])

    def forward_step(previous, inputs):
        right, lower, pivot = inputs
        current = apply_block(pivot, right - apply_block(lower, previous))
        return (current, current)

    inputs = (
        jnp.moveaxis(advected[:, 1:], 1, 0),
        jnp.moveaxis(lower_blocks, 2, 0),
        jnp.moveaxis(pivot_inverse[:, :, 1:], 2, 0),
    )
    last, rest = lax.scan(forward_step, first, inputs)
    forward = jnp.concatenate([first[None], rest], axis=0)

    def backward_step(following, inputs):
        current_forward, upper = inputs
        current = current_forward - apply_block(upper, following)
        return (current, current)

    top, lower_rest = lax.scan(
        backward_step, last, (forward[:-1], jnp.moveaxis(upper_blocks, 2, 0)), reverse=True
    )
    solved = jnp.concatenate([lower_rest, last[None]], axis=0)
    return jnp.moveaxis(solved, 0, 1)


def body(fields, east_courant, north_courant, offsets, lower_blocks, pivot_inverse, upper_blocks):
    cycle_count = lax.axis_size("lon")
    cycle_place = lax.axis_index("lon")
    band_place = lax.axis_index("lat")
    row_count = fields.shape[2]
    width = fields.shape[3]
    field_count = fields.shape[0]
    displace = jnp.mod(offsets, cycle_count)
    wanted = jnp.mod(cycle_place - displace, cycle_count)
    piece = lax.all_gather(fields, "lon", axis=3, tiled=True)
    span = piece.shape[3]
    begin = wanted * width
    valid = (begin >= 0) & (begin <= span - width)
    safe = jnp.clip(begin, 0, span - width)

    def one_row(block, anchor):
        return lax.dynamic_slice_in_dim(block, anchor, width, 2)

    taken = jax.vmap(one_row, in_axes=(2, 0), out_axes=2)(piece, safe)
    moved = jnp.where(valid[None, None, :, None], taken, 0.0)
    global_rows = band_place * row_count + jnp.arange(row_count, dtype=jnp.int32)
    total_rows = row_count * lax.axis_size("lat")
    north_wall = jnp.where((global_rows == total_rows - 1)[None, :, None], 0.0, north_courant)
    lat_stack = jnp.concatenate([moved, north_wall[None]], axis=0)
    lon_stack = jnp.concatenate([moved, east_courant[None]], axis=0)
    lat_padded = padded(lat_stack, (("lat", 2),), 1, False)
    lon_padded = padded(lon_stack, (("lon", 3),), 1, True)
    east_flux = (
        jnp.maximum(east_courant, 0.0) * moved
        + jnp.minimum(east_courant, 0.0) * lon_padded[:field_count, :, :, 2:]
    )
    west_courant = lon_padded[field_count, :, :, :-2]
    west_flux = (
        jnp.maximum(west_courant, 0.0) * lon_padded[:field_count, :, :, :-2]
        + jnp.minimum(west_courant, 0.0) * moved
    )
    north_flux = (
        jnp.maximum(north_wall, 0.0) * moved
        + jnp.minimum(north_wall, 0.0) * lat_padded[:field_count, :, 2:, :]
    )
    south_courant = lat_padded[field_count, :, :-2, :]
    south_flux = (
        jnp.maximum(south_courant, 0.0) * lat_padded[:field_count, :, :-2, :]
        + jnp.minimum(south_courant, 0.0) * moved
    )
    advected = moved - (east_flux - west_flux) - (north_flux - south_flux)
    return column_solve(advected, lower_blocks, pivot_inverse, upper_blocks)


def solution(mesh):
    in_specs = (
        P(None, None, "lat", "lon"),
        P(None, "lat", "lon"),
        P(None, "lat", "lon"),
        P("lat"),
        P(None, None, None, "lat"),
        P(None, None, None, "lat"),
        P(None, None, None, "lat"),
    )
    out_specs = P(None, None, "lat", "lon")
    return jax.shard_map(body, mesh=mesh, in_specs=in_specs, out_specs=out_specs, check_vma=False)
```

profile of v0, /device:TPU:62, one launch (start us, length us, event | category | flops | bytes accessed | tf_op | source)
XLA Modules:
  0.0 152.5 jit_solution(4412390770514833927)
XLA Ops:
  6.5 1.7 %copy.14 = f32[5,32,1,256]{3,0,2,1:T(8,128)} copy(f32[5,32,1,256]{3,2,1,0:T(1,128)} %param.11) | data formatting | bytes 327680 | tf_op args[0]
  9.0 0.8 slice.53
  9.8 0.8 copy.31
  10.7 0.1 copy.17
  10.8 0.9 copy.16
  11.7 0.9 copy.18
  12.5 0.8 broadcast_maximum_fusion.2
  13.3 0.8 broadcast_maximum_fusion.1
  14.2 88.7 %all-gather.2.cloned.1.call-done = f32[5,32,1,4096]{3,0,2,1:T(8,128)} async-done(((f32[5,32,1,256]{3,0,2,1:T(8,128)}), f32[5,32,1,4096]{3,0,2,1:T(8,128)}) %all-gather.2.cloned.1.call-update) | async-done | bytes 2621456 | tf_op jit(solution)/shard_map/all_gather | solution.py:63
  102.9 1.1 dynamic-slice_select_fusion
  104.1 0.9 fusion.25
  104.9 4.4 %collective-permute-start.1 = (f32[6,32,1,1]{3,0,2,1:T(8,128)S(1)}, f32[6,32,1,1]{3,0,2,1:T(8,128)S(1)}, u32[]{:S(2)}, u32[]{:S(2)}) collective-permute-start(f32[6,32,1,1]{3,0,2,1:T(8,128)S(1)} %get-tuple-element.182), channel_id=1, source_target_pairs={{0,1},{1,2},{2,3},{3,4},{4,5},{5,6},{6,7},{7,8},{8,9},{9,10},{10,1... | collective-permute-start | bytes 2312 | tf_op jit(solution)/shard_map/ppermute | solution.py:14
  109.4 1.9 %collective-permute-start.3 = (f32[6,32,1,256]{3,0,2,1:T(8,128)S(1)}, f32[6,32,1,256]{3,0,2,1:T(8,128)S(1)}, u32[]{:S(2)}, u32[]{:S(2)}) collective-permute-start(f32[6,32,1,256]{3,0,2,1:T(8,128)S(1)} %pad_maximum_fusion.4), channel_id=1, source_target_pairs={{0,16},{16,32},{32,48},{48,64},{64,80},{80,96},{96,112},{112,128},... | collective-permute-start | bytes 589832 | tf_op jit(solution)/shard_map/ppermute | solution.py:14
  111.3 7.5 %collective-permute-start.2 = (f32[6,32,1,256]{3,0,2,1:T(8,128)S(1)}, f32[6,32,1,256]{3,0,2,1:T(8,128)S(1)}, u32[]{:S(2)}, u32[]{:S(2)}) collective-permute-start(f32[6,32,1,256]{3,0,2,1:T(8,128)S(1)} %pad_maximum_fusion.4), channel_id=1, source_target_pairs={{16,0},{32,16},{48,32},{64,48},{80,64},{96,80},{112,96},{128,112},... | collective-permute-start | bytes 589832 | tf_op jit(solution)/shard_map/ppermute | solution.py:17
  118.9 1.9 %collective-permute-start = (f32[6,32,1,1]{3,0,2,1:T(8,128)S(1)}, f32[6,32,1,1]{3,0,2,1:T(8,128)S(1)}, u32[]{:S(2)}, u32[]{:S(2)}) collective-permute-start(f32[6,32,1,1]{3,0,2,1:T(8,128)S(1)} %get-tuple-element.181), channel_id=1, source_target_pairs={{1,0},{2,1},{3,2},{4,3},{5,4},{6,5},{7,6},{8,7},{9,8},{10,9},{11,1... | collective-permute-start | bytes 2312 | tf_op jit(solution)/shard_map/ppermute | solution.py:17
  120.8 1.0 broadcast_maximum_fusion
  121.8 0.8 collective-permute-done.3
  122.7 6.9 %collective-permute-done = f32[6,32,1,1]{3,0,2,1:T(8,128)S(1)} collective-permute-done((f32[6,32,1,1]{3,0,2,1:T(8,128)S(1)}, f32[6,32,1,1]{3,0,2,1:T(8,128)S(1)}, u32[]{:S(2)}, u32[]{:S(2)}) %collective-permute-start) | collective-permute-done | bytes 800 | tf_op jit(solution)/shard_map/ppermute | solution.py:17
  129.6 0.4 fusion.17
  130.2 8.8 %while.29 = (s32[]{:T(128)}, f32[5,1,256]{2,0,1:T(8,128)S(1)}, f32[31,5,1,256]{3,1,2,0:T(8,128)S(1)}, f32[31,5,1,256]{3,1,2,0:T(8,128)S(1)}, f32[31,5,5,1]{2,1,3...) while((s32[]{:T(128)}, f32[5,1,256]{2,0,1:T(8,128)S(1)}, f32[31,5,1,256]{3,1,2,0:T(8,128)S(1)}, ...), condition=%wide.region_1.2_spmd, body=%wide.region_0.1_spmd.sunk | while | flops 154882 | bytes 56397 | solution.py:39
  130.5 0.1 fusion.40
  130.8 0.1 fusion.40
  139.1 5.7 %while.30 = (s32[]{:T(128)}, f32[5,1,256]{2,0,1:T(8,128)S(1)}, f32[31,5,1,256]{3,2,0,1:T(1,128)S(1)}, f32[31,5,1,256]{3,1,2,0:T(8,128)S(1)}, f32[31,5,5,1]{2,1,3,0:T(8,128)S(1)}, /*index=5*/s32[]{:T(128)}, s32[]{:T(128)}) while((s32[]{:T(128)}, f32[5,1,256]{2,0,1:T(8,128)S(1)}, f32[31,5,1,256]{3,2,0,1:T(1,128)S(1)}, ...), condition=%wide.region_3.4_spmd, body=%wide.region_2.3_spmd.sunk | while | flops 78083 | bytes 50269 | solution.py:47
  144.8 0.8 maximum_bitcast_fusion
  (173 shorter events, 13.7 us)
Async XLA Ops:
  6.5 123.1 %copy-start = (f32[32,1,256]{2,1,0:T(1,128)S(1)}, f32[32,1,256]{2,1,0:T(1,128)}, u32[]{:S(2)}) copy-start(f32[32,1,256]{2,1,0:T(1,128)} %param.12) | copy-start | bytes 98308
  6.5 96.4 %all-gather.2.cloned.1.call-start = ((), (), s32[]{:S(2)}) async-start(), calls=%async_computation | async-start | bytes 4456448 | tf_op jit(solution)/shard_map/all_gather | solution.py:63
  104.9 15.8 %collective-permute-start.1 = (f32[6,32,1,1]{3,0,2,1:T(8,128)S(1)}, f32[6,32,1,1]{3,0,2,1:T(8,128)S(1)}, u32[]{:S(2)}, u32[]{:S(2)}) collective-permute-start(f32[6,32,1,1]{3,0,2,1:T(8,128)S(1)} %get-tuple-element.182), channel_id=1, source_target_pairs={{0,1},{1,2},{2,3},{3,4},{4,5},{5,6},{6,7},{7,8},{8,9},{9,10},{10,1... | collective-permute-start | bytes 2312 | tf_op jit(solution)/shard_map/ppermute | solution.py:14
  109.4 13.3 %collective-permute-start.3 = (f32[6,32,1,256]{3,0,2,1:T(8,128)S(1)}, f32[6,32,1,256]{3,0,2,1:T(8,128)S(1)}, u32[]{:S(2)}, u32[]{:S(2)}) collective-permute-start(f32[6,32,1,256]{3,0,2,1:T(8,128)S(1)} %pad_maximum_fusion.4), channel_id=1, source_target_pairs={{0,16},{16,32},{32,48},{48,64},{64,80},{80,96},{96,112},{112,128},... | collective-permute-start | bytes 589832 | tf_op jit(solution)/shard_map/ppermute | solution.py:14
  111.3 18.3 %collective-permute-start.2 = (f32[6,32,1,256]{3,0,2,1:T(8,128)S(1)}, f32[6,32,1,256]{3,0,2,1:T(8,128)S(1)}, u32[]{:S(2)}, u32[]{:S(2)}) collective-permute-start(f32[6,32,1,256]{3,0,2,1:T(8,128)S(1)} %pad_maximum_fusion.4), channel_id=1, source_target_pairs={{16,0},{32,16},{48,32},{64,48},{80,64},{96,80},{112,96},{128,112},... | collective-permute-start | bytes 589832 | tf_op jit(solution)/shard_map/ppermute | solution.py:17
  118.9 10.8 %collective-permute-start = (f32[6,32,1,1]{3,0,2,1:T(8,128)S(1)}, f32[6,32,1,1]{3,0,2,1:T(8,128)S(1)}, u32[]{:S(2)}, u32[]{:S(2)}) collective-permute-start(f32[6,32,1,1]{3,0,2,1:T(8,128)S(1)} %get-tuple-element.181), channel_id=1, source_target_pairs={{1,0},{2,1},{3,2},{4,3},{5,4},{6,5},{7,6},{8,7},{9,8},{10,9},{11,1... | collective-permute-start | bytes 2312 | tf_op jit(solution)/shard_map/ppermute | solution.py:17
Sparse Core Ops, SparseCore 0:
  9.4 93.4 all-gather.1
where the time goes:
time: 153 us; the launch traced here: 152 us
  waiting for transfers between devices  96.5 us (63%)
  starting transfers between devices  15.8 us (10%)
  between operations  14.3 us (9%)
  matrix products  13.1 us (9%)
  other arithmetic  6.02 us (4%)
  local copies, waits for them, and re-layouts  5.95 us (4%)
    all_gather x1, waiting for transfers between devices, body(): piece = lax.all_gather(fields, 'lon', axis=3, tiled=True)  88.7 us
    dot_general x94, matrix products, apply_block(): jnp.einsum('abj,bji->aji', block, vector, precision=lax.Precision.HIGHEST)  13.1 us
    ppermute x2, starting transfers between devices, padded(): lax.ppermute(lax.slice_in_dim(block, 0, width, axis=dim), axis, backward)  9.47 us
    ppermute x2, waiting for transfers between devices, padded(): lax.ppermute(lax.slice_in_dim(block, 0, width, axis=dim), axis, backward)  6.91 us
    ppermute x2, starting transfers between devices, padded(): lax.ppermute(lax.slice_in_dim(block, block.shape[dim] - width, None, axis...  6.28 us
    unnamed x11, local copies, waits for them, and re-layouts  4.32 us
  transfers between devices with their start and end apart: 5, of which 3 were waited for; matrix products, arithmetic and copies ran while one was open for 4% of the time, Pallas kernels for 0%

commit v1 on v0

--- a/solution.py
+++ b/solution.py
@@ -60,7 +60,9 @@
     field_count = fields.shape[0]
     displace = jnp.mod(offsets, cycle_count)
     wanted = jnp.mod(cycle_place - displace, cycle_count)
-    piece = lax.all_gather(fields, "lon", axis=3, tiled=True)
+    piece = jnp.concatenate(
+        lax.all_to_all(jnp.stack([fields] * lax.axis_size("lon"), axis=0), "lon", 0, 0), axis=3
+    )
     span = piece.shape[3]
     begin = wanted * width
     valid = (begin >= 0) & (begin <= span - width)

time: 153 us -> 117 us (0.76)
  the two profiles are of different devices: /device:TPU:62 before, /device:TPU:235 now
where the time goes in v1:
time: 117 us; the launch traced here: 116 us
  waiting for transfers between devices  65.4 us (56%)
  starting transfers between devices  24.5 us (21%)
  matrix products  12.5 us (11%)
  local copies, waits for them, and re-layouts  10.3 us (9%)
  other arithmetic  1.36 us (1%)
  loops' own time  1.17 us (1%)
    all_to_all x1, waiting for transfers between devices, body(): lax.all_to_all(jnp.stack([fields] * lax.axis_size('lon'), axis=0), 'lon',...  54.3 us
    ppermute x2, starting transfers between devices, padded(): lax.ppermute(lax.slice_in_dim(block, block.shape[dim] - width, None, axis...  15.1 us
    dot_general x94, matrix products, apply_block(): jnp.einsum('abj,bji->aji', block, vector, precision=lax.Precision.HIGHEST)  12.5 us
    ppermute x2, waiting for transfers between devices, padded(): lax.ppermute(lax.slice_in_dim(block, 0, width, axis=dim), axis, backward)  6.68 us
    all_to_all x1, starting transfers between devices, body(): lax.all_to_all(jnp.stack([fields] * lax.axis_size('lon'), axis=0), 'lon',...  5.56 us
    ppermute x2, waiting for transfers between devices, padded(): lax.ppermute(lax.slice_in_dim(block, block.shape[dim] - width, None, axis...  4.47 us
    ppermute x2, starting transfers between devices, padded(): lax.ppermute(lax.slice_in_dim(block, 0, width, axis=dim), axis, backward)  3.84 us
    reshape x1, local copies, waits for them, and re-layouts, body(): jnp.concatenate(lax.all_to_all(jnp.stack([fields] * lax.axis_size('lon'),...  2.99 us
  transfers between devices with their start and end apart: 5, of which 3 were waited for; matrix products, arithmetic and copies ran while one was open for 1% of the time, Pallas kernels for 0%

profile of v1, /device:TPU:235, one launch (start us, length us, event | category | flops | bytes accessed | tf_op | source)
XLA Modules:
  0.0 116.3 jit_solution(6270621349394675919)
XLA Ops:
  0.0 0.9 copy.61
  0.9 1.8 %stack.2 = f32[16,5,32,1,256]{4,2,1,3,0:T(8,128)} broadcast(f32[5,32,256]{2,1,0:T(8,128)S(1)} %bitcast.137), dimensions={1,2,4} | broadcast | bytes 2785280 | tf_op jit(solution)/shard_map/stack | solution.py:64
  2.8 5.6 %all-to-all-start = ((f32[16,5,32,1,256]{4,2,1,3,0:T(8,128)}), f32[16,5,32,1,256]{4,2,1,3,0:T(8,128)S(1)}, u32[]{:S(2)}, u32[]{:S(2)}) async-start(f32[16,5,32,1,256]{4,2,1,3,0:T(8,128)} %stack.2), calls=%async_computation | async-start | bytes 5242880 | tf_op jit(solution)/shard_map/all_to_all | solution.py:64
  9.3 0.2 copy.29
  9.4 0.2 copy.30
  9.6 0.1 copy.32
  9.8 54.3 %all-to-all-done = f32[16,5,32,1,256]{4,2,1,3,0:T(8,128)S(1)} async-done(((f32[16,5,32,1,256]{4,2,1,3,0:T(8,128)}), f32[16,5,32,1,256]{4,2,1,3,0:T(8,128)S(1)}, u32[]{:S(2)}, u32[]{:S(2)}) %all-to-all-start) | async-done | bytes 2621472 | tf_op jit(solution)/shard_map/all_to_all | solution.py:64
  64.1 3.0 %copy.24 = f32[5,32,1,16,256]{4,3,1,0,2:T(8,128)} copy(f32[5,32,1,16,256]{4,1,0,2,3:T(8,128)S(1)} %bitcast.134) | data formatting | bytes 5242880 | tf_op jit(solution)/shard_map/reshape | solution.py:63
  67.1 2.6 %transpose_reshape.3 = f32[1,5,32,4096]{3,2,1,0:T(8,128)S(1)} reshape(f32[5,32,1,16,256]{4,3,1,0,2:T(8,128)} %copy.24) | data formatting | bytes 5242880 | tf_op jit(solution)/shard_map/vmap()/transpose;reshape | solution.py:72
  69.9 6.1 %collective-permute-start.1 = (f32[6,32,1,1]{3,1,0,2:T(8,128)S(1)}, f32[6,32,1,1]{3,1,0,2:T(8,128)S(1)}, u32[]{:S(2)}, u32[]{:S(2)}) collective-permute-start(f32[6,32,1,1]{3,1,0,2:T(8,128)S(1)} %get-tuple-element.196), channel_id=1, source_target_pairs={{0,1},{1,2},{2,3},{3,4},{4,5},{5,6},{6,7},{7,8},{8,9},{9,10},{10,1... | collective-permute-start | bytes 2312 | tf_op jit(solution)/shard_map/ppermute | solution.py:14
  76.0 9.1 %collective-permute-start.3 = (f32[6,32,1,256]{3,1,0,2:T(8,128)S(1)}, f32[6,32,1,256]{3,1,0,2:T(8,128)S(1)}, u32[]{:S(2)}, u32[]{:S(2)}) collective-permute-start(f32[6,32,1,256]{3,1,0,2:T(8,128)S(1)} %pad_maximum_fusion.1), channel_id=1, source_target_pairs={{0,16},{16,32},{32,48},{48,64},{64,80},{80,96},{96,112},{112,128},... | collective-permute-start | bytes 589832 | tf_op jit(solution)/shard_map/ppermute | solution.py:14
  85.1 1.9 %collective-permute-start.2 = (f32[6,32,1,256]{3,1,0,2:T(8,128)S(1)}, f32[6,32,1,256]{3,1,0,2:T(8,128)S(1)}, u32[]{:S(2)}, u32[]{:S(2)}) collective-permute-start(f32[6,32,1,256]{3,1,0,2:T(8,128)S(1)} %pad_maximum_fusion.1), channel_id=1, source_target_pairs={{16,0},{32,16},{48,32},{64,48},{80,64},{96,80},{112,96},{128,112},... | collective-permute-start | bytes 589832 | tf_op jit(solution)/shard_map/ppermute | solution.py:17
  87.0 1.9 %collective-permute-start = (f32[6,32,1,1]{3,1,0,2:T(8,128)S(1)}, f32[6,32,1,1]{3,1,0,2:T(8,128)S(1)}, u32[]{:S(2)}, u32[]{:S(2)}) collective-permute-start(f32[6,32,1,1]{3,1,0,2:T(8,128)S(1)} %get-tuple-element.195), channel_id=1, source_target_pairs={{1,0},{2,1},{3,2},{4,3},{5,4},{6,5},{7,6},{8,7},{9,8},{10,9},{11,1... | collective-permute-start | bytes 2312 | tf_op jit(solution)/shard_map/ppermute | solution.py:17
  89.0 4.5 %collective-permute-done.3 = f32[6,32,1,256]{3,1,0,2:T(8,128)S(1)} collective-permute-done((f32[6,32,1,256]{3,1,0,2:T(8,128)S(1)}, f32[6,32,1,256]{3,1,0,2:T(8,128)S(1)}, u32[]{:S(2)}, u32[]{:S(2)}) %collective-permute-start.3) | collective-permute-done | bytes 196640 | tf_op jit(solution)/shard_map/ppermute | solution.py:14
  93.5 6.7 %collective-permute-done.2 = f32[6,32,1,256]{3,1,0,2:T(8,128)S(1)} collective-permute-done((f32[6,32,1,256]{3,1,0,2:T(8,128)S(1)}, f32[6,32,1,256]{3,1,0,2:T(8,128)S(1)}, u32[]{:S(2)}, u32[]{:S(2)}) %collective-permute-start.2) | collective-permute-done | bytes 196640 | tf_op jit(solution)/shard_map/ppermute | solution.py:17
  100.2 0.2 fusion.17
  100.6 9.2 %while.29 = (s32[]{:T(128)}, f32[5,1,256]{2,0,1:T(8,128)S(1)}, f32[31,5,1,256]{3,1,2,0:T(8,128)S(1)}, f32[31,5,1,256]{3,0,1,2:T(8,128)S(1)}, f32[31,5,5,1]{2,1,3...) while((s32[]{:T(128)}, f32[5,1,256]{2,0,1:T(8,128)S(1)}, f32[31,5,1,256]{3,1,2,0:T(8,128)S(1)}, ...), condition=%wide.region_1.2_spmd, body=%wide.region_0.1_spmd.sunk | while | flops 154882 | bytes 62557 | solution.py:39
  102.1 0.1 fusion.43
  103.8 0.1 fusion.43
  105.6 0.1 fusion.43
  107.7 0.1 fusion.43
  109.4 0.1 fusion.43
  109.9 5.6 %while.30 = (s32[]{:T(128)}, f32[5,1,256]{2,0,1:T(8,128)S(1)}, f32[31,5,1,256]{3,2,0,1:T(1,128)S(1)}, f32[31,5,1,256]{3,1,2,0:T(8,128)S(1)}, f32[31,5,5,1]{2,1,3,0:T(8,128)S(1)}, /*index=5*/s32[]{:T(128)}, s32[]{:T(128)}) while((s32[]{:T(128)}, f32[5,1,256]{2,0,1:T(8,128)S(1)}, f32[31,5,1,256]{3,2,0,1:T(1,128)S(1)}, ...), condition=%wide.region_3.4_spmd, body=%wide.region_2.3_spmd.sunk | while | flops 78083 | bytes 50277 | solution.py:47
  115.5 0.8 maximum_bitcast_fusion
  (211 shorter events, 13.7 us)
Async XLA Ops:
  2.8 6.3 %copy-start = (f32[5,5,32,1]{2,3,1,0:T(1,128)S(1)}, f32[5,5,32,1]{2,3,1,0:T(1,128)}, u32[]{:S(2)}) copy-start(f32[5,5,32,1]{2,3,1,0:T(1,128)} %param.16) | copy-start | bytes 9604
  2.8 6.5 %copy-start.3 = (f32[5,5,31,1]{2,3,1,0:T(1,128)S(1)}, f32[5,5,31,1]{2,3,1,0:T(1,128)}, u32[]{:S(2)}) copy-start(f32[5,5,31,1]{2,3,1,0:T(1,128)} %param.15) | copy-start | bytes 9304
  2.8 6.8 %copy-start.4 = (f32[5,5,31,1]{2,3,1,0:T(1,128)S(1)}, f32[5,5,31,1]{2,3,1,0:T(1,128)}, u32[]{:S(2)}) copy-start(f32[5,5,31,1]{2,3,1,0:T(1,128)} %param.17) | copy-start | bytes 9304
  2.8 7.0 %copy-start.1 = (f32[32,1,256]{2,1,0:T(1,128)S(1)}, f32[32,1,256]{2,1,0:T(1,128)}, u32[]{:S(2)}) copy-start(f32[32,1,256]{2,1,0:T(1,128)} %param.12) | copy-start | bytes 98308
  2.8 7.0 %copy-start.2 = (f32[32,1,256]{2,1,0:T(1,128)S(1)}, f32[32,1,256]{2,1,0:T(1,128)}, u32[]{:S(2)}) copy-start(f32[32,1,256]{2,1,0:T(1,128)} %param.13) | copy-start | bytes 98308
  2.8 61.3 %all-to-all-start = ((f32[16,5,32,1,256]{4,2,1,3,0:T(8,128)}), f32[16,5,32,1,256]{4,2,1,3,0:T(8,128)S(1)}, u32[]{:S(2)}, u32[]{:S(2)}) async-start(f32[16,5,32,1,256]{4,2,1,3,0:T(8,128)} %stack.2), calls=%async_computation | async-start | bytes 5242880 | tf_op jit(solution)/shard_map/all_to_all | solution.py:64
  69.9 19.0 %collective-permute-start.1 = (f32[6,32,1,1]{3,1,0,2:T(8,128)S(1)}, f32[6,32,1,1]{3,1,0,2:T(8,128)S(1)}, u32[]{:S(2)}, u32[]{:S(2)}) collective-permute-start(f32[6,32,1,1]{3,1,0,2:T(8,128)S(1)} %get-tuple-element.196), channel_id=1, source_target_pairs={{0,1},{1,2},{2,3},{3,4},{4,5},{5,6},{6,7},{7,8},{8,9},{9,10},{10,1... | collective-permute-start | bytes 2312 | tf_op jit(solution)/shard_map/ppermute | solution.py:14
  76.0 17.5 %collective-permute-start.3 = (f32[6,32,1,256]{3,1,0,2:T(8,128)S(1)}, f32[6,32,1,256]{3,1,0,2:T(8,128)S(1)}, u32[]{:S(2)}, u32[]{:S(2)}) collective-permute-start(f32[6,32,1,256]{3,1,0,2:T(8,128)S(1)} %pad_maximum_fusion.1), channel_id=1, source_target_pairs={{0,16},{16,32},{32,48},{48,64},{64,80},{80,96},{96,112},{112,128},... | collective-permute-start | bytes 589832 | tf_op jit(solution)/shard_map/ppermute | solution.py:14
  85.1 15.1 %collective-permute-start.2 = (f32[6,32,1,256]{3,1,0,2:T(8,128)S(1)}, f32[6,32,1,256]{3,1,0,2:T(8,128)S(1)}, u32[]{:S(2)}, u32[]{:S(2)}) collective-permute-start(f32[6,32,1,256]{3,1,0,2:T(8,128)S(1)} %pad_maximum_fusion.1), channel_id=1, source_target_pairs={{16,0},{32,16},{48,32},{64,48},{80,64},{96,80},{112,96},{128,112},... | collective-permute-start | bytes 589832 | tf_op jit(solution)/shard_map/ppermute | solution.py:17
  87.0 6.5 %collective-permute-start = (f32[6,32,1,1]{3,1,0,2:T(8,128)S(1)}, f32[6,32,1,1]{3,1,0,2:T(8,128)S(1)}, u32[]{:S(2)}, u32[]{:S(2)}) collective-permute-start(f32[6,32,1,1]{3,1,0,2:T(8,128)S(1)} %get-tuple-element.195), channel_id=1, source_target_pairs={{1,0},{2,1},{3,2},{4,3},{5,4},{6,5},{7,6},{8,7},{9,8},{10,9},{11,1... | collective-permute-start | bytes 2312 | tf_op jit(solution)/shard_map/ppermute | solution.py:17
